TPU v7x, 32 devices: a whole 2x2x4 slice. The times are simulated.
32 devices in a mesh: layer: 8 (over y, x, core), lat: 4 (over z).
Axes of the slice: x: 2, y: 2, z: 4, core: 2. Of those that a mesh axis runs over, the one named last changes fastest.
Arguments:
- activations: bfloat16 [1536, 4096], P('layer', 'lat'), may hold values from -6 to 6
- w_enc: bfloat16 [1536, 8192], P('layer', 'lat'), may hold values from -0.15625 to 0.15625
- w_dec: bfloat16 [1536, 8192], P('layer', 'lat'), may hold values from -0.25 to 0.25
- b_enc: bfloat16 [8192], P('lat'), may hold values from -3 to 3
- b_dec: float32 [1536], P('layer'), may hold values from -3 to 3
- tile_ids: int32 [4, 4], replicated, may hold values from -1 to 63, as said below
Outputs:
- d_w_enc: bfloat16 [1536, 8192], P('layer', 'lat')
- d_w_dec: bfloat16 [1536, 8192], P('layer', 'lat')
- d_b_enc: float32 [8192], P('lat')
Inputs may be any that keep to these rules, and one draw needn't show every extreme that they name: `tile_ids`: row b lists the tiles of block b: live ids first, then -1. Live ids of a row are distinct, and no two of them share an owner id // 16. Each row has at least half of 4 (rounded up) live slots; some row has 4. One owner is named in every row.
All inputs are finite; a program needn't handle non-finite values.
Results may differ from a plain program's by a relative error of at most 0.02.
The roundings to bfloat16 on the way count: a program that leaves them out, or rounds other values in their place, can miss the bound.
Values may be sent and summed in bfloat16 or wider, within the bound.
No kernel may reach another device: no remote copies, remote signals or barrier semaphores. Data moves between devices by JAX's collectives and lax.ppermute only.
A program may use at most 64 MiB of HBM per device.

v0:
```python
import math
import jax
import jax.numpy as jnp
from jax import lax
from jax.sharding import PartitionSpec as P

TILE = 128


def rounded(value):
    return lax.optimization_barrier(value.astype(jnp.bfloat16)).astype(jnp.float32)


def local(activations, w_enc, w_dec, b_enc, b_dec, tile_ids):
    feature_count, row_count = activations.shape
    latent_count = w_enc.shape[1]
    owner_count = lax.axis_size("lat")
    tile_count = latent_count // TILE
    position = lax.axis_index("lat")
    owner_ids = jnp.where(tile_ids >= 0, tile_ids // tile_count, -1)
    matched = owner_ids == position
    local_tile = jnp.sum(jnp.where(matched, tile_ids % tile_count, 0), axis=1)
    wanted = jnp.any(matched, axis=1)
    chosen = (local_tile[:, None] == jnp.arange(tile_count)[None, :]) & wanted[:, None]
    chosen_half = chosen.astype(jnp.bfloat16)
    enc_table = w_enc.reshape(feature_count, tile_count, TILE)
    dec_table = w_dec.reshape(feature_count, tile_count, TILE)
    bias_table = b_enc.reshape(tile_count, TILE)
    enc_send = jnp.einsum(
        "rt,ftc->rfc", chosen_half, enc_table, preferred_element_type=jnp.float32
    ).astype(jnp.bfloat16)
    dec_send = jnp.einsum(
        "rt,ftc->rfc", chosen_half, dec_table, preferred_element_type=jnp.float32
    ).astype(jnp.bfloat16)
    bias_send = jnp.dot(chosen_half, bias_table, preferred_element_type=jnp.float32).astype(
        jnp.bfloat16
    )
    enc_recv, dec_recv, bias_recv = (
        lax.all_to_all(enc_send, "lat", split_axis=0, concat_axis=0, tiled=True),
        lax.all_to_all(dec_send, "lat", split_axis=0, concat_axis=0, tiled=True),
        lax.all_to_all(bias_send, "lat", split_axis=0, concat_axis=0, tiled=True),
    )
    my_list = lax.dynamic_index_in_dim(tile_ids, position, 0, keepdims=False)
    live_slot = my_list >= 0
    source = jnp.where(live_slot, my_list // tile_count, 0)
    live_half = live_slot.astype(jnp.bfloat16)
    live_float = live_slot.astype(jnp.float32)
    enc_cols = jnp.take(enc_recv, source, axis=0) * live_half[:, None, None]
    bias_cols = jnp.take(bias_recv, source, axis=0).astype(jnp.float32)
    partial_value = rounded(
        jnp.einsum("fr,kfc->rkc", activations, enc_cols, preferred_element_type=jnp.float32)
    )
    preact = lax.psum(partial_value, "layer") + bias_cols[None]
    latent_codes = (jax.nn.relu(preact) * live_float[None, :, None]).astype(jnp.bfloat16)
    dec_cols = jnp.take(dec_recv, source, axis=0) * live_half[:, None, None]
    rebuilt = (
        jnp.einsum("rkc,kfc->fr", latent_codes, dec_cols, preferred_element_type=jnp.float32)
        + b_dec[:, None]
    )
    residual = rebuilt - activations.astype(jnp.float32)
    grad_err = (residual / math.sqrt(row_count)).astype(jnp.bfloat16)
    dec_grad = jnp.einsum(
        "fr,rkc->kfc", grad_err, latent_codes, preferred_element_type=jnp.float32
    ).astype(jnp.bfloat16)
    back_part = rounded(
        jnp.einsum("fr,kfc->rkc", grad_err, dec_cols, preferred_element_type=jnp.float32)
    )
    grad_total = lax.psum(back_part, "layer")
    code_grad = (grad_total * (latent_codes > 0)).astype(jnp.bfloat16)
    enc_grad = jnp.einsum(
        "fr,rkc->kfc", activations, code_grad, preferred_element_type=jnp.float32
    ).astype(jnp.bfloat16)
    bias_grad = jnp.sum(code_grad, axis=0, dtype=jnp.float32).astype(jnp.bfloat16)
    placement = ((source[:, None] == jnp.arange(owner_count)[None, :]) & live_slot[:, None]).astype(
        jnp.bfloat16
    )
    enc_return = jnp.einsum(
        "ko,kfc->ofc", placement, enc_grad, preferred_element_type=jnp.float32
    ).astype(jnp.bfloat16)
    dec_return = jnp.einsum(
        "ko,kfc->ofc", placement, dec_grad, preferred_element_type=jnp.float32
    ).astype(jnp.bfloat16)
    bias_return = jnp.einsum(
        "ko,kc->oc", placement, bias_grad, preferred_element_type=jnp.float32
    ).astype(jnp.bfloat16)
    enc_got, dec_got, bias_got = (
        lax.all_to_all(enc_return, "lat", split_axis=0, concat_axis=0, tiled=True),
        lax.all_to_all(dec_return, "lat", split_axis=0, concat_axis=0, tiled=True),
        lax.all_to_all(bias_return, "lat", split_axis=0, concat_axis=0, tiled=True),
    )
    d_w_enc = (
        jnp.einsum("rt,rfc->ftc", chosen_half, enc_got, preferred_element_type=jnp.float32)
        .reshape(feature_count, latent_count)
        .astype(jnp.bfloat16)
    )
    d_w_dec = (
        jnp.einsum("rt,rfc->ftc", chosen_half, dec_got, preferred_element_type=jnp.float32)
        .reshape(feature_count, latent_count)
        .astype(jnp.bfloat16)
    )
    d_b_enc = jnp.einsum(
        "rt,rc->tc", chosen_half, bias_got, preferred_element_type=jnp.float32
    ).reshape(latent_count)
    return (d_w_enc, d_w_dec, d_b_enc)


def solution(mesh):
    return jax.shard_map(
        local,
        mesh=mesh,
        in_specs=(
            P("layer", "lat"),
            P("layer", "lat"),
            P("layer", "lat"),
            P("lat"),
            P("layer"),
            P(),
        ),
        out_specs=(P("layer", "lat"), P("layer", "lat"), P("lat")),
        check_vma=False,
    )
```

profile of v0, /device:TPU:0, one launch (start us, length us, event | category | flops | bytes accessed | tf_op | source)
XLA Modules:
  0.0 188.2 jit_solution(17841347270297134224)
XLA Ops:
  7.2 0.9 fusion.44
  8.1 0.8 fusion.23
  8.9 0.1 fusion.26
  9.0 0.1 fusion.8
  9.1 0.6 copy.46
  9.7 6.3 %all-to-all-start.1 = ((bf16[4,1,128]{2,1,0:T(2,128)(2,1)}), bf16[4,1,128]{2,1,0:T(2,128)(2,1)S(1)}, u32[]{:S(2)}, u32[]{:S(2)}) async-start(bf16[4,1,128]{2,1,0:T(2,128)(2,1)} %copy.46), calls=%async_computation.1 | async-start | bytes 4096 | tf_op jit(solution)/shard_map/all_to_all | solution.py:41
  16.0 0.7 fusion.42
  16.7 0.7 compare_and_fusion
  17.5 1.3 copy.65
  18.8 0.3 convolution_convert_fusion.7
  19.0 0.2 copy.66
  19.2 0.3 convolution_convert_fusion.6
  19.5 0.7 fusion.35
  20.2 0.7 copy.45
  20.9 0.7 copy.47
  21.6 5.1 %all-to-all-start = ((bf16[4,192,128]{2,1,0:T(8,128)(2,1)}), bf16[4,192,128]{2,1,0:T(8,128)(2,1)S(1)}, u32[]{:S(2)}, u32[]{:S(2)}) async-start(bf16[4,192,128]{2,1,0:T(8,128)(2,1)} %copy.45), calls=%async_computation | async-start | bytes 393216 | tf_op jit(solution)/shard_map/all_to_all | solution.py:39
  26.7 0.6 gather_fusion
  27.3 0.1 select_convert_fusion.1
  27.3 6.6 %all-to-all-done = bf16[4,192,128]{2,1,0:T(8,128)(2,1)S(1)} async-done(((bf16[4,192,128]{2,1,0:T(8,128)(2,1)}), bf16[4,192,128]{2,1,0:T(8,128)(2,1)S(1)}, u32[]{:S(2)}, u32[]{:S(2)}) %all-to-all-start) | async-done | bytes 196640 | tf_op jit(solution)/shard_map/all_to_all | solution.py:39
  34.0 3.4 %all-to-all-start.2 = ((bf16[4,192,128]{2,1,0:T(8,128)(2,1)}), bf16[4,192,128]{2,1,0:T(8,128)(2,1)S(1)}, u32[]{:S(2)}, u32[]{:S(2)}) async-start(bf16[4,192,128]{2,1,0:T(8,128)(2,1)} %copy.47), calls=%async_computation.2 | async-start | bytes 393216 | tf_op jit(solution)/shard_map/all_to_all | solution.py:40
  37.3 0.0 all-reduce.3.cloned.1.call-start
  37.4 0.6 gather_fusion.1
  38.0 0.6 fusion
  38.6 56.5 %all-reduce.4 = f32[1024,4,128]{0,2,1:T(8,128)S(1)} all-reduce(bf16[1024,4,128]{0,2,1:T(8,128)(2,1)S(1)} %fusion), channel_id=1, replica_groups=mesh['layer'=8,'lat'=4] {'layer'}, use_global_device_ids=true, to_apply=%region_2.4 | all-reduce | flops 524288 | bytes 3145728 | tf_op jit(solution)/shard_map/psum | solution.py:53
  95.1 0.3 multiply_convert_fusion
  95.4 1.2 gather_fusion.2
  96.7 1.6 fusion.5
  98.3 1.6 convolution_convert_fusion
  99.9 0.5 fusion.7
  100.4 1.0 convolution_convert_fusion.8
  101.4 0.7 copy.56
  102.1 5.0 %all-to-all-start.4 = ((bf16[4,192,128]{2,1,0:T(8,128)(2,1)}), bf16[4,192,128]{2,1,0:T(8,128)(2,1)S(1)}, u32[]{:S(2)}, u32[]{:S(2)}) async-start(bf16[4,192,128]{2,1,0:T(8,128)(2,1)} %copy.56), calls=%async_computation.4 | async-start | bytes 393216 | tf_op jit(solution)/shard_map/all_to_all | solution.py:88
  107.1 49.9 %all-reduce.3.cloned.1.call-done = bf16[1024,4,128]{0,2,1:T(8,128)(2,1)} async-done(((bf16[1024,4,128]{0,2,1:T(8,128)(2,1)}), bf16[1024,4,128]{0,2,1:T(8,128)(2,1)}) %all-reduce.3.cloned.1.call-update) | async-done | bytes 1048592 | tf_op jit(solution)/shard_map/psum | solution.py:68
  157.0 2.0 %fusion.41 = bf16[4,128]{1,0:T(4,128)(2,1)S(1)} fusion(bf16[1024,4,128]{0,2,1:T(8,128)(2,1)} %all-reduce.3.cloned.1.call-done, f32[4]{0:T(128)S(1)} %copy-done.9, f32[1024,4,128]{0,2,1:T(8,128)S(1)} %all-reduce.4, f32[4,128]{1,0:T(4,128)S(1)} %select_convert_fusion.1), kind=kLoop, calls=%fused_computation.90 | loop fusion | flops 4718080 | bytes 3148816 | tf_op jit(solution)/shard_map/reduce_sum | solution.py:73
  158.9 0.1 fusion.9
  159.1 0.6 copy.58
  159.7 0.5 fusion.6
  160.2 4.5 %all-to-all-start.5 = ((bf16[4,1,128]{2,1,0:T(2,128)(2,1)}), bf16[4,1,128]{2,1,0:T(2,128)(2,1)S(1)}, u32[]{:S(2)}, u32[]{:S(2)}) async-start(bf16[4,1,128]{2,1,0:T(2,128)(2,1)} %copy.58), calls=%async_computation.5 | async-start | bytes 4096 | tf_op jit(solution)/shard_map/all_to_all | solution.py:89
  164.7 0.3 convolution_convert_fusion.9
  165.0 0.7 copy.52
  165.7 4.5 %all-to-all-done.5 = bf16[4,1,128]{2,1,0:T(2,128)(2,1)S(1)} async-done(((bf16[4,1,128]{2,1,0:T(2,128)(2,1)}), bf16[4,1,128]{2,1,0:T(2,128)(2,1)S(1)}, u32[]{:S(2)}, u32[]{:S(2)}) %all-to-all-start.5) | async-done | bytes 1056 | tf_op jit(solution)/shard_map/all_to_all | solution.py:89
  170.2 3.4 %all-to-all-start.3 = ((bf16[4,192,128]{2,1,0:T(8,128)(2,1)}), bf16[4,192,128]{2,1,0:T(8,128)(2,1)S(1)}, u32[]{:S(2)}, u32[]{:S(2)}) async-start(bf16[4,192,128]{2,1,0:T(8,128)(2,1)} %copy.52), calls=%async_computation.3 | async-start | bytes 393216 | tf_op jit(solution)/shard_map/all_to_all | solution.py:87
  173.6 0.4 convolution_convert_fusion.2
  174.0 1.1 copy.84
  175.1 0.8 convolution_bitcast_fusion.1
  175.9 3.9 %all-to-all-done.3 = bf16[4,192,128]{2,1,0:T(8,128)(2,1)S(1)} async-done(((bf16[4,192,128]{2,1,0:T(8,128)(2,1)}), bf16[4,192,128]{2,1,0:T(8,128)(2,1)S(1)}, u32[]{:S(2)}, u32[]{:S(2)}) %all-to-all-start.3) | async-done | bytes 196640 | tf_op jit(solution)/shard_map/all_to_all | solution.py:87
  179.8 0.4 convolution_convert_fusion.3
  180.2 1.1 copy.85
  (36 shorter events, 0.1 us)
Async XLA Ops:
  7.2 1.8 copy-start
  7.2 11.8 %copy-start.2 = (bf16[192,2048]{1,0:T(8,128)(2,1)S(1)}, bf16[192,2048]{1,0:T(8,128)(2,1)}, u32[]{:S(2)}) copy-start(bf16[192,2048]{1,0:T(8,128)(2,1)} %param.10) | copy-start | bytes 2359300
  9.7 11.9 %all-to-all-start.1 = ((bf16[4,1,128]{2,1,0:T(2,128)(2,1)}), bf16[4,1,128]{2,1,0:T(2,128)(2,1)S(1)}, u32[]{:S(2)}, u32[]{:S(2)}) async-start(bf16[4,1,128]{2,1,0:T(2,128)(2,1)} %copy.46), calls=%async_computation.1 | async-start | bytes 4096 | tf_op jit(solution)/shard_map/all_to_all | solution.py:41
  16.7 2.8 %copy-start.10 = (pred[4]{0:T(512)(128)(4,1)}, pred[4]{0:T(512)(128)(4,1)S(1)}, u32[]{:S(2)}) copy-start(pred[4]{0:T(512)(128)(4,1)S(1)} %get-tuple-element.5) | copy-start | bytes 16
  16.7 78.4 %copy-start.8 = (f32[4]{0:T(128)}, f32[4]{0:T(128)S(1)}, u32[]{:S(2)}) copy-start(f32[4]{0:T(128)S(1)} %get-tuple-element.4) | copy-start | bytes 52
  17.4 1.8 copy-start.12
  17.4 78.0 %copy-start.6 = (bf16[4]{0:T(256)(128)(2,1)}, bf16[4]{0:T(256)(128)(2,1)S(1)}, u32[]{:S(2)}) copy-start(bf16[4]{0:T(256)(128)(2,1)S(1)} %get-tuple-element.10) | copy-start | bytes 28
  19.0 19.0 %copy-start.4 = (bf16[192,1024]{1,0:T(8,128)(2,1)S(1)}, bf16[192,1024]{1,0:T(8,128)(2,1)}, u32[]{:S(2)}) copy-start(bf16[192,1024]{1,0:T(8,128)(2,1)} %param.8) | copy-start | bytes 1179652
  21.6 12.4 %all-to-all-start = ((bf16[4,192,128]{2,1,0:T(8,128)(2,1)}), bf16[4,192,128]{2,1,0:T(8,128)(2,1)S(1)}, u32[]{:S(2)}, u32[]{:S(2)}) async-start(bf16[4,192,128]{2,1,0:T(8,128)(2,1)} %copy.45), calls=%async_computation | async-start | bytes 393216 | tf_op jit(solution)/shard_map/all_to_all | solution.py:39
  34.0 61.4 %all-to-all-start.2 = ((bf16[4,192,128]{2,1,0:T(8,128)(2,1)}), bf16[4,192,128]{2,1,0:T(8,128)(2,1)S(1)}, u32[]{:S(2)}, u32[]{:S(2)}) async-start(bf16[4,192,128]{2,1,0:T(8,128)(2,1)} %copy.47), calls=%async_computation.2 | async-start | bytes 393216 | tf_op jit(solution)/shard_map/all_to_all | solution.py:40
  37.3 119.6 %all-reduce.3.cloned.1.call-start = ((), (), s32[]{:S(2)}) async-start(), calls=%async_computation.6 | async-start | bytes 2097152 | tf_op jit(solution)/shard_map/psum | solution.py:68
  96.7 1.6 copy-start.3
  96.7 1.6 copy-start.7
  99.9 57.1 %copy-start.9 = (f32[4]{0:T(128)S(1)}, f32[4]{0:T(128)}, u32[]{:S(2)}) copy-start(f32[4]{0:T(128)} %copy-done.8) | copy-start | bytes 52
  100.4 58.5 %copy-start.11 = (pred[4]{0:T(512)(128)(4,1)S(1)}, pred[4]{0:T(512)(128)(4,1)}, u32[]{:S(2)}) copy-start(pred[4]{0:T(512)(128)(4,1)} %copy-done.10) | copy-start | bytes 16
  100.4 58.5 %copy-start.13 = (s32[4]{0:T(128)S(1)}, s32[4]{0:T(128)}, u32[]{:S(2)}) copy-start(s32[4]{0:T(128)} %copy-done.12) | copy-start | bytes 52
  102.1 58.1 %all-to-all-start.4 = ((bf16[4,192,128]{2,1,0:T(8,128)(2,1)}), bf16[4,192,128]{2,1,0:T(8,128)(2,1)S(1)}, u32[]{:S(2)}, u32[]{:S(2)}) async-start(bf16[4,192,128]{2,1,0:T(8,128)(2,1)} %copy.56), calls=%async_computation.4 | async-start | bytes 393216 | tf_op jit(solution)/shard_map/all_to_all | solution.py:88
  156.9 2.7 %copy-start.1 = (bf16[1024,4,128]{0,2,1:T(8,128)(2,1)S(1)}, bf16[1024,4,128]{0,2,1:T(8,128)(2,1)}, u32[]{:S(2)}) copy-start(bf16[1024,4,128]{0,2,1:T(8,128)(2,1)} %all-reduce.3.cloned.1.call-done) | copy-start | bytes 3145732
  156.9 2.7 %copy-start.5 = (bf16[192,1024]{1,0:T(8,128)(2,1)S(1)}, bf16[192,1024]{1,0:T(8,128)(2,1)}, u32[]{:S(2)}) copy-start(bf16[192,1024]{1,0:T(8,128)(2,1)} %param.8) | copy-start | bytes 1179652
  160.2 10.0 %all-to-all-start.5 = ((bf16[4,1,128]{2,1,0:T(2,128)(2,1)}), bf16[4,1,128]{2,1,0:T(2,128)(2,1)S(1)}, u32[]{:S(2)}, u32[]{:S(2)}) async-start(bf16[4,1,128]{2,1,0:T(2,128)(2,1)} %copy.58), calls=%async_computation.5 | async-start | bytes 4096 | tf_op jit(solution)/shard_map/all_to_all | solution.py:89
  170.2 9.6 %all-to-all-start.3 = ((bf16[4,192,128]{2,1,0:T(8,128)(2,1)}), bf16[4,192,128]{2,1,0:T(8,128)(2,1)S(1)}, u32[]{:S(2)}, u32[]{:S(2)}) async-start(bf16[4,192,128]{2,1,0:T(8,128)(2,1)} %copy.52), calls=%async_computation.3 | async-start | bytes 393216 | tf_op jit(solution)/shard_map/all_to_all | solution.py:87
Sparse Core Ops, SparseCore 0:
  100.0 56.8 all-reduce.2
where the time goes:
time: 189 us; the launch traced here: 188 us
  waiting for transfers between devices  65 us (34%)
  blocking collectives  56.5 us (30%)
  starting transfers between devices  27.7 us (15%)
  between operations  14.3 us (8%)
  local copies, waits for them, and re-layouts  10.1 us (5%)
  matrix products  8.36 us (4%)
  other arithmetic  6.22 us (3%)
    psum x1, blocking collectives, local(): preact = lax.psum(partial_value, 'layer') + bias_cols[None]  56.5 us
    psum x1, waiting for transfers between devices, local(): grad_total = lax.psum(back_part, 'layer')  49.9 us
    all_to_all x1, waiting for transfers between devices, local(): lax.all_to_all(enc_send, 'lat', split_axis=0, concat_axis=0, tiled=True)  6.63 us
    all_to_all x1, starting transfers between devices, local(): lax.all_to_all(bias_send, 'lat', split_axis=0, concat_axis=0, tiled=True)  6.35 us
    all_to_all x1, starting transfers between devices, local(): lax.all_to_all(enc_send, 'lat', split_axis=0, concat_axis=0, tiled=True)  5.09 us
    all_to_all x1, starting transfers between devices, local(): lax.all_to_all(dec_return, 'lat', split_axis=0, concat_axis=0, tiled=True)  4.97 us
    all_to_all x1, starting transfers between devices, local(): lax.all_to_all(bias_return, 'lat', split_axis=0, concat_axis=0, tiled=True)  4.55 us
    all_to_all x1, waiting for transfers between devices, local(): lax.all_to_all(bias_return, 'lat', split_axis=0, concat_axis=0, tiled=True)  4.53 us
  transfers between devices with their start and end apart: 7, of which 4 were waited for; matrix products, arithmetic and copies ran while one was open for 9% of the time, Pallas kernels for 0%

commit v1 on v0

--- a/solution.py
+++ b/solution.py
@@ -50,7 +50,7 @@
     partial_value = rounded(
         jnp.einsum("fr,kfc->rkc", activations, enc_cols, preferred_element_type=jnp.float32)
     )
-    preact = lax.psum(partial_value, "layer") + bias_cols[None]
+    preact = jnp.sum(lax.all_gather(partial_value, "layer"), axis=0) + bias_cols[None]
     latent_codes = (jax.nn.relu(preact) * live_float[None, :, None]).astype(jnp.bfloat16)
     dec_cols = jnp.take(dec_recv, source, axis=0) * live_half[:, None, None]
     rebuilt = (

time: 189 us -> 243 us (1.29)
  waiting for transfers between devices: 65 us -> 143 us
  blocking collectives: 56.5 us -> 0 us
  local copies, waits for them, and re-layouts: 10.1 us -> 34.3 us
  other arithmetic: 6.22 us -> 16.5 us
    all_gather x0 -> x1, waiting for transfers between devices: none -> 68.7 us  [local(): lax.all_gather(partial_value, 'layer')]
    psum x1 -> x0, blocking collectives: 56.5 us -> none  [local(): preact = lax.psum(partial_value, 'layer') + bias_cols[None]]
    unnamed x33 -> x38, local copies, waits for them, and re-layouts: 3.68 us -> 26.1 us
    reduce_sum x0 -> x1, other arithmetic: none -> 9.65 us  [local(): jnp.sum(lax.all_gather(partial_value, 'layer'), axis=0) + bias_cols[None]]
    all_to_all x1, waiting for transfers between devices: 0.01 us -> 5.5 us  [local(): lax.all_to_all(dec_send, 'lat', split_axis=0, concat_axis=0, tiled=True)]
    all_to_all x1, waiting for transfers between devices: 0.01 us -> 4.3 us  [local(): lax.all_to_all(bias_send, 'lat', split_axis=0, concat_axis=0, tiled=True)]
    all_to_all x1, starting transfers between devices: 6.35 us -> 3.22 us  [local(): lax.all_to_all(bias_send, 'lat', split_axis=0, concat_axis=0, tiled=True)]
  transfers between devices with their start and end apart: 7 -> 8, of which waited for: 4 -> 7; matrix products, arithmetic and copies ran while one was open for 9% -> 6% of each run, Pallas kernels for 0% -> 0%
where the time goes in v1:
time: 243 us; the launch traced here: 242 us
  waiting for transfers between devices  143 us (59%)
  local copies, waits for them, and re-layouts  34.3 us (14%)
  starting transfers between devices  25.5 us (10%)
  other arithmetic  16.5 us (7%)
  between operations  14.4 us (6%)
  matrix products  8.55 us (4%)
    all_gather x1, waiting for transfers between devices, local(): lax.all_gather(partial_value, 'layer')  68.7 us
    psum x1, waiting for transfers between devices, local(): grad_total = lax.psum(back_part, 'layer')  49.3 us
    unnamed x38, local copies, waits for them, and re-layouts  26.1 us
    reduce_sum x1, other arithmetic, local(): jnp.sum(lax.all_gather(partial_value, 'layer'), axis=0) + bias_cols[None]  9.65 us
    all_to_all x1, waiting for transfers between devices, local(): lax.all_to_all(enc_send, 'lat', split_axis=0, concat_axis=0, tiled=True)  6.44 us
    all_to_all x1, starting transfers between devices, local(): lax.all_to_all(enc_send, 'lat', split_axis=0, concat_axis=0, tiled=True)  6.35 us
    all_to_all x1, waiting for transfers between devices, local(): lax.all_to_all(dec_send, 'lat', split_axis=0, concat_axis=0, tiled=True)  5.5 us
  transfers between devices with their start and end apart: 8, of which 7 were waited for; matrix products, arithmetic and copies ran while one was open for 6% of the time, Pallas kernels for 0%

profile of v1, /device:TPU:0, one launch (start us, length us, event | category | flops | bytes accessed | tf_op | source)
XLA Modules:
  0.0 242.0 jit_solution(9959865610316527451)
XLA Ops:
  7.2 0.9 fusion.44
  8.1 0.8 fusion.23
  8.9 1.3 copy.48
  10.2 0.3 convolution_convert_fusion.7
  10.5 0.7 copy.35
  11.2 6.3 %all-to-all-start = ((bf16[4,192,128]{2,1,0:T(8,128)(2,1)}), bf16[4,192,128]{2,1,0:T(8,128)(2,1)S(1)}, u32[]{:S(2)}, u32[]{:S(2)}) async-start(bf16[4,192,128]{2,1,0:T(8,128)(2,1)} %copy.35), calls=%async_computation | async-start | bytes 393216 | tf_op jit(solution)/shard_map/all_to_all | solution.py:39
  17.6 0.5 fusion.42
  18.1 0.5 copy-done.11
  18.6 6.4 %all-to-all-done = bf16[4,192,128]{2,1,0:T(8,128)(2,1)S(1)} async-done(((bf16[4,192,128]{2,1,0:T(8,128)(2,1)}), bf16[4,192,128]{2,1,0:T(8,128)(2,1)S(1)}, u32[]{:S(2)}, u32[]{:S(2)}) %all-to-all-start) | async-done | bytes 196640 | tf_op jit(solution)/shard_map/all_to_all | solution.py:39
  25.1 0.6 gather_fusion.1
  25.7 0.6 fusion
  26.3 1.6 all_gather.12
  28.0 0.6 copy.36
  28.6 3.2 %all-to-all-start.1 = ((bf16[4,1,128]{2,1,0:T(2,128)(2,1)}), bf16[4,1,128]{2,1,0:T(2,128)(2,1)S(1)}, u32[]{:S(2)}, u32[]{:S(2)}) async-start(bf16[4,1,128]{2,1,0:T(2,128)(2,1)} %copy.36), calls=%async_computation.1 | async-start | bytes 4096 | tf_op jit(solution)/shard_map/all_to_all | solution.py:41
  32.3 0.7 copy.38
  33.0 4.3 %all-to-all-done.1 = bf16[4,1,128]{2,1,0:T(2,128)(2,1)S(1)} async-done(((bf16[4,1,128]{2,1,0:T(2,128)(2,1)}), bf16[4,1,128]{2,1,0:T(2,128)(2,1)S(1)}, u32[]{:S(2)}, u32[]{:S(2)}) %all-to-all-start.1) | async-done | bytes 1056 | tf_op jit(solution)/shard_map/all_to_all | solution.py:41
  37.3 3.4 %all-to-all-start.2 = ((bf16[4,192,128]{2,1,0:T(8,128)(2,1)}), bf16[4,192,128]{2,1,0:T(8,128)(2,1)S(1)}, u32[]{:S(2)}, u32[]{:S(2)}) async-start(bf16[4,192,128]{2,1,0:T(8,128)(2,1)} %copy.38), calls=%async_computation.2 | async-start | bytes 393216 | tf_op jit(solution)/shard_map/all_to_all | solution.py:40
  40.7 0.6 gather_fusion
  41.4 5.5 %all-to-all-done.2 = bf16[4,192,128]{2,1,0:T(8,128)(2,1)S(1)} async-done(((bf16[4,192,128]{2,1,0:T(8,128)(2,1)}), bf16[4,192,128]{2,1,0:T(8,128)(2,1)S(1)}, u32[]{:S(2)}, u32[]{:S(2)}) %all-to-all-start.2) | async-done | bytes 196640 | tf_op jit(solution)/shard_map/all_to_all | solution.py:40
  46.9 1.2 gather_fusion.2
  48.1 68.7 %all-gather.3.cloned.1.call-done = f32[8192,4,128]{0,2,1:T(8,128)} async-done(((f32[1024,4,128]{0,2,1:T(8,128)}), f32[8192,4,128]{0,2,1:T(8,128)}) %all-gather.3.cloned.1.call-update) | async-done | bytes 16777232 | tf_op jit(solution)/shard_map/all_gather | solution.py:53
  116.8 21.2 %copy.49 = f32[64,8,8,1024]{3,2,1,0:T(8,128)} copy(f32[64,8,8,1024]{3,1,2,0:T(8,128)} %bitcast.109) | data formatting | bytes 33554432
  138.0 9.7 %reduce_sum.31 = f32[1024,4,128]{0,2,1:T(8,128)} reduce(f32[8,1024,4,128]{1,0,3,2:T(8,128)} %bitcast.108, f32[]{:T(128)} %constant.81.clone.1), dimensions={0}, to_apply=%region_2.4 | reduce | flops 3670016 | bytes 18874372 | tf_op jit(solution)/shard_map/reduce_sum | solution.py:53
  147.6 1.9 copy.37
  149.6 1.0 multiply_convert_fusion
  150.6 0.5 fusion.5
  151.1 0.7 copy-done.5
  151.9 1.5 convolution_convert_fusion
  153.4 1.4 fusion.7
  154.8 0.9 convolution_convert_fusion.8
  155.7 0.7 copy.43
  156.4 4.6 %all-to-all-start.4 = ((bf16[4,192,128]{2,1,0:T(8,128)(2,1)}), bf16[4,192,128]{2,1,0:T(8,128)(2,1)S(1)}, u32[]{:S(2)}, u32[]{:S(2)}) async-start(bf16[4,192,128]{2,1,0:T(8,128)(2,1)} %copy.43), calls=%async_computation.4 | async-start | bytes 393216 | tf_op jit(solution)/shard_map/all_to_all | solution.py:88
  161.0 49.3 %all-reduce.2.cloned.1.call-done = bf16[1024,4,128]{2,0,1:T(8,128)(2,1)} async-done(((bf16[1024,4,128]{2,0,1:T(8,128)(2,1)}), bf16[1024,4,128]{2,0,1:T(8,128)(2,1)}) %all-reduce.2.cloned.1.call-update) | async-done | bytes 1048592 | tf_op jit(solution)/shard_map/psum | solution.py:68
  210.3 1.9 fusion.41
  212.2 0.8 fusion.9
  213.0 0.6 copy.45
  213.6 0.4 fusion.6
  214.0 4.5 %all-to-all-start.5 = ((bf16[4,1,128]{2,1,0:T(2,128)(2,1)}), bf16[4,1,128]{2,1,0:T(2,128)(2,1)S(1)}, u32[]{:S(2)}, u32[]{:S(2)}) async-start(bf16[4,1,128]{2,1,0:T(2,128)(2,1)} %copy.45), calls=%async_computation.5 | async-start | bytes 4096 | tf_op jit(solution)/shard_map/all_to_all | solution.py:89
  218.5 0.3 convolution_convert_fusion.9
  218.8 0.7 copy.40
  219.5 4.5 %all-to-all-done.5 = bf16[4,1,128]{2,1,0:T(2,128)(2,1)S(1)} async-done(((bf16[4,1,128]{2,1,0:T(2,128)(2,1)}), bf16[4,1,128]{2,1,0:T(2,128)(2,1)S(1)}, u32[]{:S(2)}, u32[]{:S(2)}) %all-to-all-start.5) | async-done | bytes 1056 | tf_op jit(solution)/shard_map/all_to_all | solution.py:89
  224.0 3.4 %all-to-all-start.3 = ((bf16[4,192,128]{2,1,0:T(8,128)(2,1)}), bf16[4,192,128]{2,1,0:T(8,128)(2,1)S(1)}, u32[]{:S(2)}, u32[]{:S(2)}) async-start(bf16[4,192,128]{2,1,0:T(8,128)(2,1)} %copy.40), calls=%async_computation.3 | async-start | bytes 393216 | tf_op jit(solution)/shard_map/all_to_all | solution.py:87
  227.4 0.4 convolution_convert_fusion.2
  227.8 1.1 copy.69
  228.9 0.8 convolution_bitcast_fusion.1
  229.7 3.9 %all-to-all-done.3 = bf16[4,192,128]{2,1,0:T(8,128)(2,1)S(1)} async-done(((bf16[4,192,128]{2,1,0:T(8,128)(2,1)}), bf16[4,192,128]{2,1,0:T(8,128)(2,1)S(1)}, u32[]{:S(2)}, u32[]{:S(2)}) %all-to-all-start.3) | async-done | bytes 196640 | tf_op jit(solution)/shard_map/all_to_all | solution.py:87
  233.6 0.4 convolution_convert_fusion.3
  234.0 1.1 copy.70
  (46 shorter events, 0.9 us)
Async XLA Ops:
  7.2 20.7 %copy-start = (bf16[2048]{0:T(1024)(128)(2,1)S(1)}, bf16[2048]{0:T(1024)(128)(2,1)}, u32[]{:S(2)}) copy-start(bf16[2048]{0:T(1024)(128)(2,1)} %param.11) | copy-start | bytes 12292
  7.2 10.4 %copy-start.7 = (s32[4,4]{1,0:T(4,128)S(1)}, s32[4,4]{1,0:T(4,128)}, u32[]{:S(2)}) copy-start(s32[4,4]{1,0:T(4,128)} %param.13) | copy-start | bytes 196
  7.2 18.5 %copy-start.3 = (bf16[192,1024]{1,0:T(8,128)(2,1)S(1)}, bf16[192,1024]{1,0:T(8,128)(2,1)}, u32[]{:S(2)}) copy-start(bf16[192,1024]{1,0:T(8,128)(2,1)} %param.8) | copy-start | bytes 1179652
  11.2 13.9 %all-to-all-start = ((bf16[4,192,128]{2,1,0:T(8,128)(2,1)}), bf16[4,192,128]{2,1,0:T(8,128)(2,1)S(1)}, u32[]{:S(2)}, u32[]{:S(2)}) async-start(bf16[4,192,128]{2,1,0:T(8,128)(2,1)} %copy.35), calls=%async_computation | async-start | bytes 393216 | tf_op jit(solution)/shard_map/all_to_all | solution.py:39
  17.6 99.2 %all-gather.3.cloned.1.call-start = ((), (), s32[]{:S(2)}) async-start(), calls=%async_computation.7 | async-start | bytes 18874368 | tf_op jit(solution)/shard_map/all_gather | solution.py:53
  18.1 0.5 copy-start.11
  18.1 0.5 copy-start.13
  18.1 9.7 %copy-start.9 = (bf16[4]{0:T(256)(128)(2,1)}, bf16[4]{0:T(256)(128)(2,1)S(1)}, u32[]{:S(2)}) copy-start(bf16[4]{0:T(256)(128)(2,1)S(1)} %get-tuple-element.10) | copy-start | bytes 28
  26.2 5.6 %copy-start.2 = (bf16[192,2048]{1,0:T(8,128)(2,1)S(1)}, bf16[192,2048]{1,0:T(8,128)(2,1)}, u32[]{:S(2)}) copy-start(bf16[192,2048]{1,0:T(8,128)(2,1)} %param.10) | copy-start | bytes 2359300
  28.6 8.7 %all-to-all-start.1 = ((bf16[4,1,128]{2,1,0:T(2,128)(2,1)}), bf16[4,1,128]{2,1,0:T(2,128)(2,1)S(1)}, u32[]{:S(2)}, u32[]{:S(2)}) async-start(bf16[4,1,128]{2,1,0:T(2,128)(2,1)} %copy.36), calls=%async_computation.1 | async-start | bytes 4096 | tf_op jit(solution)/shard_map/all_to_all | solution.py:41
  37.3 9.6 %all-to-all-start.2 = ((bf16[4,192,128]{2,1,0:T(8,128)(2,1)}), bf16[4,192,128]{2,1,0:T(8,128)(2,1)S(1)}, u32[]{:S(2)}, u32[]{:S(2)}) async-start(bf16[4,192,128]{2,1,0:T(8,128)(2,1)} %copy.38), calls=%async_computation.2 | async-start | bytes 393216 | tf_op jit(solution)/shard_map/all_to_all | solution.py:40
  40.6 169.6 %all-reduce.2.cloned.1.call-start = ((), (), s32[]{:S(2)}) async-start(), calls=%async_computation.6 | async-start | bytes 2097152 | tf_op jit(solution)/shard_map/psum | solution.py:68
  149.5 1.0 copy-start.6
  149.5 1.0 copy-start.10
  149.5 1.0 copy-start.15
  151.1 0.7 copy-start.5
  153.4 56.9 %copy-start.8 = (f32[4]{0:T(128)S(1)}, f32[4]{0:T(128)}, u32[]{:S(2)}) copy-start(f32[4]{0:T(128)} %get-tuple-element.4) | copy-start | bytes 52
  156.4 57.6 %all-to-all-start.4 = ((bf16[4,192,128]{2,1,0:T(8,128)(2,1)}), bf16[4,192,128]{2,1,0:T(8,128)(2,1)S(1)}, u32[]{:S(2)}, u32[]{:S(2)}) async-start(bf16[4,192,128]{2,1,0:T(8,128)(2,1)} %copy.43), calls=%async_computation.4 | async-start | bytes 393216 | tf_op jit(solution)/shard_map/all_to_all | solution.py:88
  210.3 3.3 %copy-start.1 = (bf16[1024,4,128]{2,0,1:T(8,128)(2,1)S(1)}, bf16[1024,4,128]{2,0,1:T(8,128)(2,1)}, u32[]{:S(2)}) copy-start(bf16[1024,4,128]{2,0,1:T(8,128)(2,1)} %all-reduce.2.cloned.1.call-done) | copy-start | bytes 3145732
  210.3 3.3 %copy-start.4 = (bf16[192,1024]{1,0:T(8,128)(2,1)S(1)}, bf16[192,1024]{1,0:T(8,128)(2,1)}, u32[]{:S(2)}) copy-start(bf16[192,1024]{1,0:T(8,128)(2,1)} %param.8) | copy-start | bytes 1179652
  212.2 6.4 %copy-start.12 = (pred[4]{0:T(512)(128)(4,1)S(1)}, pred[4]{0:T(512)(128)(4,1)}, u32[]{:S(2)}) copy-start(pred[4]{0:T(512)(128)(4,1)} %copy-done.11) | copy-start | bytes 16
  212.2 6.4 %copy-start.14 = (s32[4]{0:T(128)S(1)}, s32[4]{0:T(128)}, u32[]{:S(2)}) copy-start(s32[4]{0:T(128)} %copy-done.13) | copy-start | bytes 52
  214.0 10.0 %all-to-all-start.5 = ((bf16[4,1,128]{2,1,0:T(2,128)(2,1)}), bf16[4,1,128]{2,1,0:T(2,128)(2,1)S(1)}, u32[]{:S(2)}, u32[]{:S(2)}) async-start(bf16[4,1,128]{2,1,0:T(2,128)(2,1)} %copy.45), calls=%async_computation.5 | async-start | bytes 4096 | tf_op jit(solution)/shard_map/all_to_all | solution.py:89
  224.0 9.6 %all-to-all-start.3 = ((bf16[4,192,128]{2,1,0:T(8,128)(2,1)}), bf16[4,192,128]{2,1,0:T(8,128)(2,1)S(1)}, u32[]{:S(2)}, u32[]{:S(2)}) async-start(bf16[4,192,128]{2,1,0:T(8,128)(2,1)} %copy.40), calls=%async_computation.3 | async-start | bytes 393216 | tf_op jit(solution)/shard_map/all_to_all | solution.py:87
Sparse Core Ops, SparseCore 0:
  28.0 88.7 all-gather.2
  153.5 56.7 all-reduce.1
